TPU v7x, 32 devices: a whole 2x2x4 slice. The times are simulated.
32 devices in a mesh: dp: 8 (over z, x), tensor: 4 (over y, core).
Axes of the slice: x: 2, y: 2, z: 4, core: 2. Of those that a mesh axis runs over, the one named last changes fastest.
Arguments:
- layer_input: bfloat16 [12288, 768], P('dp'), may hold values from -6 to 6
- patch_coords: int32 [3, 12288], P(None, 'dp'), may hold values from 0 to 55, as said below
- item_lengths: int32 [32], P('dp'), may hold values from 0 to 1536, as said below
- out_grad: bfloat16 [12288, 768], P('dp'), may hold values from -6 to 6
- ln1_gain: bfloat16 [768], replicated, may hold values from 0.25 to 1.75
- ln1_shift: bfloat16 [768], replicated, may hold values from -1.75 to 1.75
- w_qkv: bfloat16 [768, 3, 768], P(None, None, 'tensor'), may hold values from -0.21875 to 0.21875
- b_qv: bfloat16 [2, 768], P(None, 'tensor'), may hold values from -3 to 3
- w_out: bfloat16 [768, 768], P('tensor'), may hold values from -0.875 to 0.875
- b_out: bfloat16 [768], replicated, may hold values from -1.75 to 1.75
- ln2_gain: bfloat16 [768], replicated, may hold values from 0.25 to 1.75
- ln2_shift: bfloat16 [768], replicated, may hold values from -1.75 to 1.75
- w_fc1: bfloat16 [768, 3072], P(None, 'tensor'), may hold values from -0.21875 to 0.21875
- b_fc1: bfloat16 [3072], P('tensor'), may hold values from -3 to 3
- w_fc2: bfloat16 [3072, 768], P('tensor'), may hold values from -0.109375 to 0.109375
- b_fc2: bfloat16 [768], replicated, may hold values from -1.75 to 1.75
Outputs:
- layer_output: bfloat16 [12288, 768], P('dp')
- input_grad: float32 [12288, 768], P('dp')
- grad_ln1_gain: float32 [768], replicated
- grad_ln1_shift: float32 [768], replicated
- grad_w_qkv: float32 [768, 3, 768], P(None, None, 'tensor')
- grad_b_qv: float32 [2, 768], P(None, 'tensor')
- grad_w_out: float32 [768, 768], P('tensor')
- grad_b_out: float32 [768], replicated
- grad_ln2_gain: float32 [768], replicated
- grad_ln2_shift: float32 [768], replicated
- grad_w_fc1: float32 [768, 3072], P(None, 'tensor')
- grad_b_fc1: float32 [3072], P('tensor')
- grad_w_fc2: float32 [3072, 768], P('tensor')
- grad_b_fc2: float32 [768], replicated
Inputs may be any that keep to these rules, and one draw needn't show every extreme that they name: `item_lengths`: A row of 8 takes 4 consecutive entries: its items' visible lengths, laid out one after another from the row's first slot, summing to at most 1536; the remaining slots are padding. In every draw some row holds a single item of 1536 tokens. `patch_coords`: row 0 is the token's frame, 0 to 2; rows 1 and 2 are its patch row and column.
All inputs are finite; a program needn't handle non-finite values.
Results may differ from a plain program's by a relative error of at most 0.018.
Values may be sent and summed in bfloat16 or wider, within the bound.
A program may use at most 128 MiB of HBM per device.

v0:
```python
from functools import partial
import math
import jax
import jax.numpy as jnp
from jax import lax
from jax.sharding import PartitionSpec as P

HEAD_DIM = 64
NORM_EPS = 1e-06
MASK_FILL = -1e30


def layer_norm(values_in, norm_gain, norm_shift):
    mean_row = jnp.mean(values_in, axis=-1, keepdims=True)
    centred = values_in - mean_row
    spread = jnp.mean(centred * centred, axis=-1, keepdims=True)
    return centred * lax.rsqrt(spread + NORM_EPS) * norm_gain + norm_shift


def sincos_table(coords, feature_count):
    half_width = feature_count // 6
    ladder = jnp.arange(half_width, dtype=jnp.float32) / half_width
    frequency = jnp.power(10000.0, -ladder)
    angles = coords.astype(jnp.float32)[:, :, None] * frequency[None, None, :]
    wave_parts = jnp.concatenate([jnp.sin(angles), jnp.cos(angles)], axis=2)
    return jnp.concatenate([wave_parts[0], wave_parts[1], wave_parts[2]], axis=1)


def item_layout(length_rows, token_count, slot_count):
    item_ends = jnp.cumsum(length_rows, axis=1, dtype=jnp.int32)
    places = jnp.arange(token_count, dtype=jnp.int32)
    passed = (places[None, :, None] >= item_ends[:, None, :]).astype(jnp.int32)
    item_of = jnp.sum(passed, axis=2, dtype=jnp.int32)
    visible = places[None, :] < item_ends[:, -1:]
    return (jnp.where(visible, item_of, slot_count + places[None, :]), visible)


def block_scores(query_block, key_rows, segment_block, segment):
    score_scale = 1.0 / math.sqrt(key_rows.shape[2])
    scores = (
        jnp.einsum("qhd,khd->hqk", query_block, key_rows, preferred_element_type=jnp.float32)
        * score_scale
    )
    allowed = (segment_block[:, None] == segment[None, :])[None]
    return jnp.where(allowed, scores, MASK_FILL)


def attend_forward(query_rows, key_rows, value_rows, segment):
    row_count = query_rows.shape[0]
    block_rows = min(512, row_count)

    def attend_block(block_index):
        block_start = block_index * block_rows
        query_block = lax.dynamic_slice_in_dim(query_rows, block_start, block_rows, 0)
        segment_block = lax.dynamic_slice_in_dim(segment, block_start, block_rows, 0)
        scores = block_scores(query_block, key_rows, segment_block, segment)
        row_max = jnp.max(scores, axis=2, keepdims=True)
        raised = jnp.exp(scores - row_max)
        row_total = jnp.sum(raised, axis=2, keepdims=True)
        weights = (raised / row_total).astype(jnp.bfloat16)
        mixed = jnp.einsum("hqk,khd->qhd", weights, value_rows, preferred_element_type=jnp.float32)
        return (mixed, (row_max + jnp.log(row_total))[:, :, 0])

    mixed_all, log_totals = lax.map(attend_block, jnp.arange(row_count // block_rows))
    return (mixed_all.reshape(query_rows.shape), log_totals)


def attend_backward(query_rows, key_rows, value_rows, segment, mixed_grad, log_totals):
    row_count = query_rows.shape[0]
    block_rows = min(512, row_count)
    score_scale = 1.0 / math.sqrt(key_rows.shape[2])
    zeros_kv = jnp.zeros(key_rows.shape, jnp.float32)

    def back_block(running, inputs):
        block_index, lse_block = inputs
        key_acc, value_acc = running
        block_start = block_index * block_rows
        query_block = lax.dynamic_slice_in_dim(query_rows, block_start, block_rows, 0)
        segment_block = lax.dynamic_slice_in_dim(segment, block_start, block_rows, 0)
        grad_block = lax.dynamic_slice_in_dim(mixed_grad, block_start, block_rows, 0)
        scores = block_scores(query_block, key_rows, segment_block, segment)
        weights = jnp.exp(scores - lse_block[:, :, None])
        weight_grad = jnp.einsum(
            "qhd,khd->hqk", grad_block, value_rows, preferred_element_type=jnp.float32
        )
        centre = jnp.sum(weights * weight_grad, axis=2, keepdims=True)
        score_grad = (weights * (weight_grad - centre)).astype(jnp.bfloat16)
        query_grad = (
            jnp.einsum("hqk,khd->qhd", score_grad, key_rows, preferred_element_type=jnp.float32)
            * score_scale
        )
        key_acc = (
            key_acc
            + jnp.einsum(
                "hqk,qhd->khd", score_grad, query_block, preferred_element_type=jnp.float32
            )
            * score_scale
        )
        value_acc = value_acc + jnp.einsum(
            "hqk,qhd->khd",
            weights.astype(jnp.bfloat16),
            grad_block,
            preferred_element_type=jnp.float32,
        )
        return ((key_acc, value_acc), query_grad)

    block_list = jnp.arange(row_count // block_rows)
    (key_grad, value_grad), query_grad = lax.scan(
        back_block, (zeros_kv, zeros_kv), (block_list, log_totals)
    )
    return (query_grad.reshape(query_rows.shape), key_grad, value_grad)


def run_forward(hidden_in, segment, visible, params, second_pass):
    (
        ln1_gain,
        ln1_shift,
        w_qkv,
        b_qv,
        w_out,
        b_out,
        ln2_gain,
        ln2_shift,
        w_fc1,
        b_fc1,
        w_fc2,
        b_fc2,
    ) = params
    row_count = hidden_in.shape[0]
    heads_here = w_out.shape[0] // HEAD_DIM
    head_shape = (row_count, heads_here, HEAD_DIM)
    normed_one = layer_norm(
        hidden_in, ln1_gain.astype(jnp.float32), ln1_shift.astype(jnp.float32)
    ).astype(jnp.bfloat16)
    projected = jnp.einsum("td,dcj->tcj", normed_one, w_qkv, preferred_element_type=jnp.float32)
    query_rows = (
        (projected[:, 0] + b_qv[0].astype(jnp.float32)).astype(jnp.bfloat16).reshape(head_shape)
    )
    key_rows = projected[:, 1].astype(jnp.bfloat16).reshape(head_shape)
    value_rows = (
        (projected[:, 2] + b_qv[1].astype(jnp.float32)).astype(jnp.bfloat16).reshape(head_shape)
    )
    mixed, log_totals = attend_forward(query_rows, key_rows, value_rows, segment)
    mixed_low = mixed.reshape(row_count, -1).astype(jnp.bfloat16)
    attn_part = jnp.dot(mixed_low, w_out, preferred_element_type=jnp.float32).astype(jnp.bfloat16)
    if second_pass:
        attn_total = lax.psum(attn_part, "tensor").astype(jnp.float32)
    else:
        attn_total = lax.psum(attn_part, "tensor").astype(jnp.float32)
    middle = hidden_in + attn_total + b_out.astype(jnp.float32)
    normed_two = layer_norm(
        middle, ln2_gain.astype(jnp.float32), ln2_shift.astype(jnp.float32)
    ).astype(jnp.bfloat16)
    hidden_pre = jnp.dot(normed_two, w_fc1, preferred_element_type=jnp.float32) + b_fc1.astype(
        jnp.float32
    )
    activated = jax.nn.gelu(hidden_pre, approximate=False).astype(jnp.bfloat16)
    kept_state = (
        normed_one,
        query_rows,
        key_rows,
        value_rows,
        log_totals,
        mixed_low,
        middle,
        normed_two,
        hidden_pre,
        activated,
    )
    if second_pass:
        return (None, kept_state)
    mlp_part = jnp.dot(activated, w_fc2, preferred_element_type=jnp.float32).astype(jnp.bfloat16)
    mlp_total = lax.psum(mlp_part, "tensor").astype(jnp.float32)
    result = jnp.where(visible[:, None], middle + mlp_total + b_fc2.astype(jnp.float32), 0.0)
    return (result, kept_state)


def sum_gradients(grads):
    large = [g.ndim == 2 and g.shape[0] > 2 or g.ndim == 3 for g in grads]
    low = lax.psum([g.astype(jnp.bfloat16) for g, w in zip(grads, large) if w], "dp")
    wide = lax.psum([g for g, w in zip(grads, large) if not w], "dp")
    return [low.pop(0).astype(jnp.float32) if w else wide.pop(0) for w in large]


def on_device(
    layer_input,
    patch_coords,
    item_lengths,
    out_grad,
    ln1_gain,
    ln1_shift,
    w_qkv,
    b_qv,
    w_out,
    b_out,
    ln2_gain,
    ln2_shift,
    w_fc1,
    b_fc1,
    w_fc2,
    b_fc2,
):
    segment_rows, visible_rows = item_layout(
        item_lengths.reshape(1, -1), layer_input.shape[0], item_lengths.shape[0]
    )
    segment = segment_rows[0]
    visible = visible_rows[0]
    hidden_in = layer_input.astype(jnp.float32) + sincos_table(patch_coords, layer_input.shape[1])
    params = (
        ln1_gain,
        ln1_shift,
        w_qkv,
        b_qv,
        w_out,
        b_out,
        ln2_gain,
        ln2_shift,
        w_fc1,
        b_fc1,
        w_fc2,
        b_fc2,
    )
    result, kept_state = run_forward(hidden_in, segment, visible, params, False)
    (
        normed_one,
        query_rows,
        key_rows,
        value_rows,
        log_totals,
        mixed_low,
        middle,
        normed_two,
        hidden_pre,
        activated,
    ) = kept_state
    top_grad = jnp.where(visible[:, None], out_grad, jnp.zeros_like(out_grad))
    top_grad_wide = top_grad.astype(jnp.float32)
    grad_b_fc2 = jnp.sum(top_grad_wide, axis=0)
    grad_w_fc2 = jnp.einsum("tf,td->fd", activated, top_grad, preferred_element_type=jnp.float32)
    act_grad = jnp.einsum("td,fd->tf", top_grad, w_fc2, preferred_element_type=jnp.float32)
    gelu_value, gelu_back = jax.vjp(partial(jax.nn.gelu, approximate=False), hidden_pre)
    pre_grad = gelu_back(act_grad)[0].astype(jnp.bfloat16)
    grad_b_fc1 = jnp.sum(pre_grad.astype(jnp.float32), axis=0)
    grad_w_fc1 = jnp.einsum("td,tf->df", normed_two, pre_grad, preferred_element_type=jnp.float32)
    norm_grad_part = jnp.einsum("tf,df->td", pre_grad, w_fc1, preferred_element_type=jnp.float32)
    norm_grad_two = lax.psum(norm_grad_part.astype(jnp.bfloat16), "tensor").astype(jnp.float32)
    unused_two, norm_back_two = jax.vjp(
        layer_norm, middle, ln2_gain.astype(jnp.float32), ln2_shift.astype(jnp.float32)
    )
    middle_ln, grad_ln2_gain, grad_ln2_shift = norm_back_two(norm_grad_two)
    middle_grad = top_grad_wide + middle_ln
    grad_b_out = jnp.sum(middle_grad, axis=0)
    middle_low = middle_grad.astype(jnp.bfloat16)
    grad_w_out = jnp.einsum("tj,td->jd", mixed_low, middle_low, preferred_element_type=jnp.float32)
    mixed_grad = (
        jnp.einsum("td,jd->tj", middle_low, w_out, preferred_element_type=jnp.float32)
        .astype(jnp.bfloat16)
        .reshape(query_rows.shape)
    )
    query_grad, key_grad, value_grad = attend_backward(
        query_rows, key_rows, value_rows, segment, mixed_grad, log_totals
    )
    row_count = query_rows.shape[0]
    proj_grad = (
        jnp.stack([query_grad, key_grad, value_grad], axis=1)
        .astype(jnp.bfloat16)
        .reshape(row_count, 3, -1)
    )
    grad_b_qv = jnp.sum(proj_grad[:, 0::2].astype(jnp.float32), axis=0)
    grad_w_qkv = jnp.einsum(
        "td,tcj->dcj", normed_one, proj_grad, preferred_element_type=jnp.float32
    )
    norm_grad_first = jnp.einsum(
        "tcj,dcj->td", proj_grad, w_qkv, preferred_element_type=jnp.float32
    )
    norm_grad_one = lax.psum(norm_grad_first.astype(jnp.bfloat16), "tensor").astype(jnp.float32)
    unused_one, norm_back_one = jax.vjp(
        layer_norm, hidden_in, ln1_gain.astype(jnp.float32), ln1_shift.astype(jnp.float32)
    )
    input_ln, grad_ln1_gain, grad_ln1_shift = norm_back_one(norm_grad_one)
    input_grad = middle_grad + input_ln
    (
        grad_ln1_gain,
        grad_ln1_shift,
        grad_w_qkv,
        grad_b_qv,
        grad_w_out,
        grad_b_out,
        grad_ln2_gain,
        grad_ln2_shift,
        grad_w_fc1,
        grad_b_fc1,
        grad_w_fc2,
        grad_b_fc2,
    ) = sum_gradients(
        (
            grad_ln1_gain,
            grad_ln1_shift,
            grad_w_qkv,
            grad_b_qv,
            grad_w_out,
            grad_b_out,
            grad_ln2_gain,
            grad_ln2_shift,
            grad_w_fc1,
            grad_b_fc1,
            grad_w_fc2,
            grad_b_fc2,
        )
    )
    return (
        result.astype(jnp.bfloat16),
        input_grad,
        grad_ln1_gain,
        grad_ln1_shift,
        grad_w_qkv,
        grad_b_qv,
        grad_w_out,
        grad_b_out,
        grad_ln2_gain,
        grad_ln2_shift,
        grad_w_fc1,
        grad_b_fc1,
        grad_w_fc2,
        grad_b_fc2,
    )


def solution(mesh):
    placed = (
        P("dp", None),
        P(None, "dp"),
        P("dp"),
        P("dp", None),
        P(),
        P(),
        P(None, None, "tensor"),
        P(None, "tensor"),
        P("tensor", None),
        P(),
        P(),
        P(),
        P(None, "tensor"),
        P("tensor"),
        P("tensor", None),
        P(),
    )
    return jax.shard_map(
        on_device,
        mesh=mesh,
        in_specs=placed,
        out_specs=(
            P("dp", None),
            P("dp", None),
            P(),
            P(),
            P(None, None, "tensor"),
            P(None, "tensor"),
            P("tensor", None),
            P(),
            P(),
            P(),
            P(None, "tensor"),
            P("tensor"),
            P("tensor", None),
            P(),
        ),
        check_vma=False,
    )
```

profile of v0, /device:TPU:0, one launch (start us, length us, event | category | flops | bytes accessed | tf_op | source)
XLA Modules:
  0.0 612.9 jit_solution(17201050054439104026)
XLA Ops:
  8.1 8.3 %multiply_sine_fusion = (f32[3,1536,128]{2,1,0:T(8,128)S(1)}, f32[3,1536,128]{2,1,0:T(8,128)S(1)}) fusion(f32[128]{0:T(128)S(1)} %negate_power_fusion, f32[3,1536]{1,0:T(4,128)S(1)} %convert_element_type.153), kind=kLoop, calls=%fused_computation.89 | loop fusion | flops 589824 | bytes 4737536 | tf_op jit(solution)/shard_map/sin | solution.py:25
  29.3 39.0 %while.27 = (s32[]{:T(128)}, bf16[3,512,3,64]{1,3,2,0:T(8,128)(2,1)S(1)}, f32[3,3,512]{2,1,0:T(4,128)}, s32[3]{0:T(128)S(1)}, s32[1536]{0:T(1024)}, /*index=5*/s...) while((s32[]{:T(128)}, ...), condition=%wide.region_7.8_spmd, body=%wide.region_4.7_spmd.sunk | while | flops 633076224 | bytes 33307488 | solution.py:64
  77.6 53.4 %all-reduce.8.cloned.1.call-done = bf16[1536,768]{1,0:T(8,128)(2,1)} async-done(((bf16[1536,768]{1,0:T(8,128)(2,1)}), bf16[1536,768]{1,0:T(8,128)(2,1)}) %all-reduce.8.cloned.1.call-update) | async-done | bytes 2359312 | tf_op jit(solution)/shard_map/psum | solution.py:149
  137.1 12.8 %multiply_convert_fusion.1 = (bf16[1536,768]{1,0:T(8,128)(2,1)}, f32[1536,768]{1,0:T(8,128)S(1)}, f32[1536,768]{1,0:T(8,128)S(1)}) fusion(f32[768]{0:T(1024)S(1)} %copy-done.49, bf16[1536,768]{1,0:T(8,128)(2,1)S(1)} %add_convert_fusion.1, bf16[768,768]{1,0:T(8,128)(2,1)S(1)} %copy-done), kind=kOutput, calls=%fused_computation.69 | convolution fusion | flops 1889796096 | bytes 15338496 | tf_op jit(solution)/shard_map/dot_general | solution.py:154
  149.9 4.6 convert_reduce_fusion.3
  159.4 5.4 convolution_convert_fusion.1
  164.8 50.4 %all-reduce.10.cloned.1.call-done = bf16[1536,768]{1,0:T(8,128)(2,1)} async-done(((bf16[1536,768]{1,0:T(8,128)(2,1)}), bf16[1536,768]{1,0:T(8,128)(2,1)}) %all-reduce.10.cloned.1.call-update) | async-done | bytes 2359312 | tf_op jit(solution)/shard_map/psum | solution.py:246
  215.2 5.3 convert_reduce_fusion.1
  220.6 5.2 fusion.38
  225.8 5.2 fusion.57
  235.9 114.1 %while.28 = (s32[]{:T(128)}, f32[1536,3,64]{0,2,1:T(8,128)}, f32[1536,3,64]{0,2,1:T(8,128)S(1)}, bf16[3,512,3,64]{1,3,2,0:T(8,128)(2,1)}, s32[3]{0:T(128)S(1)}, ...) while((s32[]{:T(128)}, f32[1536,3,64]{0,2,1:T(8,128)}, ...), condition=%wide.region_17.18_spmd.clone, body=%wide.region_15.17_spmd.clone.sunk | while | flops 1533540864 | bytes 113105432 | solution.py:108
  237.1 6.0 fusion.122
  245.1 8.1 %multiply_reduce_fusion.4 = (f32[3,512]{1,0:T(4,128)S(1)}, f32[3,512,1536]{2,1,0:T(8,128)}) fusion(f32[3,512,1536]{2,1,0:T(8,128)} %fusion.122, f32[3,512]{1,0:T(4,128)S(1)} %dynamic-slice_bitcast_fusion.2, bf16[1536,3,64]{0,2,1:T(8,128)(2,1)S(1)} %get-tuple-element.476, bf16[1536,3,64]{0,2,1:T(8,128)(2,1)} %get-tuple-element.473, ...), kind=kOutput, calls=%fused_computation.16.clone.1 | convolution fusion | flops 313784832 | bytes 20459524 | tf_op jit(solution)/shard_map/while/body/eval_jaxpr/qhd,khd->hqk/dot_general | solution.py:41
  253.3 9.4 %multiply_convert_fusion.3 = bf16[3,512,1536]{2,1,0:T(8,128)(2,1)} fusion(f32[3,512,1536]{2,1,0:T(8,128)} %get-tuple-element.395, f32[3,512,1536]{2,1,0:T(8,128)} %fusion.122, f32[3,512]{1,0:T(4,128)S(1)} %get-tuple-element.396), kind=kLoop, calls=%fused_computation.15.clone.1 | loop fusion | flops 7077888 | bytes 23599104 | tf_op jit(solution)/shard_map/while/body/eval_jaxpr/convert_element_type | solution.py:87
  269.1 4.9 fusion.124
  275.2 6.0 fusion.122
  283.2 8.1 %multiply_reduce_fusion.4 = (f32[3,512]{1,0:T(4,128)S(1)}, f32[3,512,1536]{2,1,0:T(8,128)}) fusion(f32[3,512,1536]{2,1,0:T(8,128)} %fusion.122, f32[3,512]{1,0:T(4,128)S(1)} %dynamic-slice_bitcast_fusion.2, bf16[1536,3,64]{0,2,1:T(8,128)(2,1)S(1)} %get-tuple-element.476, bf16[1536,3,64]{0,2,1:T(8,128)(2,1)} %get-tuple-element.473, ...), kind=kOutput, calls=%fused_computation.16.clone.1 | convolution fusion | flops 313784832 | bytes 20459524 | tf_op jit(solution)/shard_map/while/body/eval_jaxpr/qhd,khd->hqk/dot_general | solution.py:41
  291.3 9.4 %multiply_convert_fusion.3 = bf16[3,512,1536]{2,1,0:T(8,128)(2,1)} fusion(f32[3,512,1536]{2,1,0:T(8,128)} %get-tuple-element.395, f32[3,512,1536]{2,1,0:T(8,128)} %fusion.122, f32[3,512]{1,0:T(4,128)S(1)} %get-tuple-element.396), kind=kLoop, calls=%fused_computation.15.clone.1 | loop fusion | flops 7077888 | bytes 23599104 | tf_op jit(solution)/shard_map/while/body/eval_jaxpr/convert_element_type | solution.py:87
  307.1 4.9 fusion.124
  313.2 6.0 fusion.122
  321.2 8.1 %multiply_reduce_fusion.4 = (f32[3,512]{1,0:T(4,128)S(1)}, f32[3,512,1536]{2,1,0:T(8,128)}) fusion(f32[3,512,1536]{2,1,0:T(8,128)} %fusion.122, f32[3,512]{1,0:T(4,128)S(1)} %dynamic-slice_bitcast_fusion.2, bf16[1536,3,64]{0,2,1:T(8,128)(2,1)S(1)} %get-tuple-element.476, bf16[1536,3,64]{0,2,1:T(8,128)(2,1)} %get-tuple-element.473, ...), kind=kOutput, calls=%fused_computation.16.clone.1 | convolution fusion | flops 313784832 | bytes 20459524 | tf_op jit(solution)/shard_map/while/body/eval_jaxpr/qhd,khd->hqk/dot_general | solution.py:41
  329.4 9.4 %multiply_convert_fusion.3 = bf16[3,512,1536]{2,1,0:T(8,128)(2,1)} fusion(f32[3,512,1536]{2,1,0:T(8,128)} %get-tuple-element.395, f32[3,512,1536]{2,1,0:T(8,128)} %fusion.122, f32[3,512]{1,0:T(4,128)S(1)} %get-tuple-element.396), kind=kLoop, calls=%fused_computation.15.clone.1 | loop fusion | flops 7077888 | bytes 23599104 | tf_op jit(solution)/shard_map/while/body/eval_jaxpr/convert_element_type | solution.py:87
  345.2 4.9 fusion.124
  354.2 4.6 bitcast_convert_fusion
  358.9 5.6 convolution_convert_fusion.5
  372.3 80.8 %all-reduce.14.cloned.1.call-done = (bf16[1536,768]{1,0:T(8,128)(2,1)}, bf16[1536,768]{1,0:T(8,128)(2,1)}) async-done(((bf16[1536,768]{1,0:T(8,128)(2,1)}, bf16[1536,768]{1,0:T(8,128)(2,1)}), (bf16[1536,768]{1,0:T(8,128)(2,1)}, bf16[1536,768]{1,0:T(8,128)(2,1)})) %all-reduce.14.cloned.1.call-update) | async-done | bytes 4718608 | tf_op jit(solution)/shard_map/psum | solution.py:173
  453.1 4.7 convert_reduce_fusion
  457.9 4.3 fusion.39
  462.3 40.5 %all-reduce = (f32[768]{0:T(1024)}, f32[768]{0:T(1024)}, f32[2,192]{1,0:T(2,128)}, f32[768]{0:T(1024)}, f32[768]{0:T(1024)}, /*index=5*/f32[768]{0:T(1024)}, f32[768]{0:T(1024)}, f32[768]{0:T(1024)}) all-reduce(f32[768]{0:T(1024)S(1)} %get-tuple-element.172, ...), channel_id=1, replica_groups=mesh['dp'=8,'tensor'=4] {'dp'}, use_global_device_ids=true, to_apply=%region_22.23 | all-reduce | flops 5760 | bytes 46080 | tf_op jit(solution)/shard_map/psum | solution.py:181
  502.9 4.8 select_convert_fusion
  508.8 4.8 add_add_fusion.2
  513.6 84.2 %all-reduce.12.cloned.1.call-done = (bf16[768,3,192]{0,2,1:T(8,128)(2,1)}, bf16[192,768]{1,0:T(8,128)(2,1)}, bf16[768,768]{1,0:T(8,128)(2,1)}, bf16[768,768]{1,0:T(8,128)(2,1)}) async-done(((bf16[768,3,192]{0,2,1:T(8,128)(2,1)}, bf16[192,768]{1,0:T(8,128)(2,1)}, bf16[768,768]{1,0:T(8,128)(2,1)}, bf16[768,768]{1,0:T(8,128)(2,1)}), (bf16[768,3,192]{0,2,1:T(8,128)(2,1)}, bf16[192,768]{1,0:T(8,128)(2,1)}, ...) | async-done | bytes 3538960 | tf_op jit(solution)/shard_map/psum | solution.py:180
  (290 shorter events, 122.7 us)
Async XLA Ops:
  7.2 129.8 %copy-start = (bf16[768,768]{1,0:T(8,128)(2,1)S(1)}, bf16[768,768]{1,0:T(8,128)(2,1)}, u32[]{:S(2)}) copy-start(bf16[768,768]{1,0:T(8,128)(2,1)} %param.32) | copy-start | bytes 3538948
  7.2 123.8 %all-reduce.8.cloned.1.call-start = ((), (), s32[]{:S(2)}) async-start(), calls=%async_computation | async-start | bytes 4718592 | tf_op jit(solution)/shard_map/psum | solution.py:149
  68.3 66.5 %copy-start.8 = (bf16[1536,3,64]{0,2,1:T(8,128)(2,1)}, bf16[1536,3,64]{0,2,1:T(8,128)(2,1)S(1)}, u32[]{:S(2)}) copy-start(bf16[1536,3,64]{0,2,1:T(8,128)(2,1)S(1)} %get-tuple-element.500) | copy-start | bytes 1769476
  69.0 65.8 %copy-start.12 = (bf16[24,8,3,512]{3,1,2,0:T(8,128)(2,1)}, bf16[24,8,3,512]{3,1,2,0:T(8,128)(2,1)S(1)}, u32[]{:S(2)}) copy-start(bf16[24,8,3,512]{3,1,2,0:T(8,128)(2,1)S(1)} %copy.35) | copy-start | bytes 1769476
  72.5 142.8 %all-reduce.10.cloned.1.call-start = ((), (), s32[]{:S(2)}) async-start(), calls=%async_computation.1 | async-start | bytes 4718592 | tf_op jit(solution)/shard_map/psum | solution.py:246
  135.5 14.3 %copy-start.38 = (f32[1536]{0:T(1024)}, f32[1536]{0:T(1024)S(1)}, u32[]{:S(2)}) copy-start(f32[1536]{0:T(1024)S(1)} %multiply_reduce_fusion.1) | copy-start | bytes 18436
  135.6 14.3 %copy-start.30 = (f32[1536]{0:T(1024)}, f32[1536]{0:T(1024)S(1)}, u32[]{:S(2)}) copy-start(f32[1536]{0:T(1024)S(1)} %fusion.53) | copy-start | bytes 18436
  137.0 12.8 %copy-start.22 = (bf16[1536,768]{1,0:T(8,128)(2,1)}, bf16[1536,768]{1,0:T(8,128)(2,1)S(1)}, u32[]{:S(2)}) copy-start(bf16[1536,768]{1,0:T(8,128)(2,1)S(1)} %add_convert_fusion.1) | copy-start | bytes 7077892
  137.0 12.8 %copy-start.17 = (bf16[1536,768]{1,0:T(8,128)(2,1)S(1)}, bf16[1536,768]{1,0:T(8,128)(2,1)}, u32[]{:S(2)}) copy-start(bf16[1536,768]{1,0:T(8,128)(2,1)} %param.23) | copy-start | bytes 7077892
  137.0 12.8 %copy-start.40 = (pred[1536]{0:T(1024)(128)(4,1)S(1)}, pred[1536]{0:T(1024)(128)(4,1)}, u32[]{:S(2)}) copy-start(pred[1536]{0:T(1024)(128)(4,1)} %iota_compare_fusion.1) | copy-start | bytes 4612
  137.1 12.8 %copy-start.55 = (bf16[768,768]{1,0:T(8,128)(2,1)S(1)}, bf16[768,768]{1,0:T(8,128)(2,1)}, u32[]{:S(2)}) copy-start(bf16[768,768]{1,0:T(8,128)(2,1)} %param.34) | copy-start | bytes 3538948
  159.4 293.7 %all-reduce.14.cloned.1.call-start = ((), (), s32[]{:S(2)}) async-start(), calls=%async_computation.3 | async-start | bytes 9437184 | tf_op jit(solution)/shard_map/psum | solution.py:173
  159.4 55.8 %copy-start.35 = (f32[768]{0:T(1024)S(1)}, f32[768]{0:T(1024)}, u32[]{:S(2)}) copy-start(f32[768]{0:T(1024)} %convert_element_type.166) | copy-start | bytes 9220
  164.8 55.8 %copy-start.39 = (f32[1536]{0:T(1024)S(1)}, f32[1536]{0:T(1024)}, u32[]{:S(2)}) copy-start(f32[1536]{0:T(1024)} %copy-done.38) | copy-start | bytes 18436
  164.8 55.8 %copy-start.31 = (f32[1536]{0:T(1024)S(1)}, f32[1536]{0:T(1024)}, u32[]{:S(2)}) copy-start(f32[1536]{0:T(1024)} %copy-done.30) | copy-start | bytes 18436
  225.8 7.5 %copy-start.23 = (bf16[192,768]{1,0:T(8,128)(2,1)S(1)}, bf16[192,768]{1,0:T(8,128)(2,1)}, u32[]{:S(2)}) copy-start(bf16[192,768]{1,0:T(8,128)(2,1)} %param.28) | copy-start | bytes 884740
  253.3 9.5 %copy-start.6 = (f32[1536,3,64]{0,2,1:T(8,128)S(1)}, f32[1536,3,64]{0,2,1:T(8,128)}, u32[]{:S(2)}) copy-start(f32[1536,3,64]{0,2,1:T(8,128)} %get-tuple-element.453) | copy-start | bytes 3538948 | tf_op jit(solution)/shard_map/while
  266.3 7.7 %copy-start.7 = (f32[1536,3,64]{0,2,1:T(8,128)}, f32[1536,3,64]{0,2,1:T(8,128)S(1)}, u32[]{:S(2)}) copy-start(f32[1536,3,64]{0,2,1:T(8,128)S(1)} %fusion.123) | copy-start | bytes 3538948 | tf_op jit(solution)/shard_map/while
  274.0 7.2 %copy-start.58 = (s32[3]{0:T(128)}, s32[3]{0:T(128)S(1)}, u32[]{:S(2)}) copy-start(s32[3]{0:T(128)S(1)} %get-tuple-element.472) | copy-start | bytes 40 | tf_op jit(solution)/shard_map/while
  291.3 9.5 %copy-start.6 = (f32[1536,3,64]{0,2,1:T(8,128)S(1)}, f32[1536,3,64]{0,2,1:T(8,128)}, u32[]{:S(2)}) copy-start(f32[1536,3,64]{0,2,1:T(8,128)} %get-tuple-element.453) | copy-start | bytes 3538948 | tf_op jit(solution)/shard_map/while
  304.3 7.7 %copy-start.7 = (f32[1536,3,64]{0,2,1:T(8,128)}, f32[1536,3,64]{0,2,1:T(8,128)S(1)}, u32[]{:S(2)}) copy-start(f32[1536,3,64]{0,2,1:T(8,128)S(1)} %fusion.123) | copy-start | bytes 3538948 | tf_op jit(solution)/shard_map/while
  312.0 7.2 %copy-start.58 = (s32[3]{0:T(128)}, s32[3]{0:T(128)S(1)}, u32[]{:S(2)}) copy-start(s32[3]{0:T(128)S(1)} %get-tuple-element.472) | copy-start | bytes 40 | tf_op jit(solution)/shard_map/while
  329.4 9.5 %copy-start.6 = (f32[1536,3,64]{0,2,1:T(8,128)S(1)}, f32[1536,3,64]{0,2,1:T(8,128)}, u32[]{:S(2)}) copy-start(f32[1536,3,64]{0,2,1:T(8,128)} %get-tuple-element.453) | copy-start | bytes 3538948 | tf_op jit(solution)/shard_map/while
  342.4 7.7 %copy-start.7 = (f32[1536,3,64]{0,2,1:T(8,128)}, f32[1536,3,64]{0,2,1:T(8,128)S(1)}, u32[]{:S(2)}) copy-start(f32[1536,3,64]{0,2,1:T(8,128)S(1)} %fusion.123) | copy-start | bytes 3538948 | tf_op jit(solution)/shard_map/while
  358.8 239.0 %all-reduce.12.cloned.1.call-start = ((), (), s32[]{:S(2)}) async-start(), calls=%async_computation.2 | async-start | bytes 7077888 | tf_op jit(solution)/shard_map/psum | solution.py:180
  370.6 82.5 %copy-start.27 = (f32[1536]{0:T(1024)S(1)}, f32[1536]{0:T(1024)}, u32[]{:S(2)}) copy-start(f32[1536]{0:T(1024)} %copy-done.26) | copy-start | bytes 18436
  370.6 82.5 %copy-start.33 = (f32[768]{0:T(1024)S(1)}, f32[768]{0:T(1024)}, u32[]{:S(2)}) copy-start(f32[768]{0:T(1024)} %copy-done.32) | copy-start | bytes 9220
  372.1 85.8 %copy-start.37 = (f32[1536]{0:T(1024)S(1)}, f32[1536]{0:T(1024)}, u32[]{:S(2)}) copy-start(f32[1536]{0:T(1024)} %copy-done.36) | copy-start | bytes 18436
  372.1 85.8 %copy-start.29 = (f32[1536]{0:T(1024)S(1)}, f32[1536]{0:T(1024)}, u32[]{:S(2)}) copy-start(f32[1536]{0:T(1024)} %copy-done.28) | copy-start | bytes 18436
  457.9 49.7 %slice-start = ((s8[4718592]{0:T(1024)(128)(4,1)}), s8[524288]{0:T(1024)(128)(4,1)S(1)}, s32[]{:S(2)}) async-start(s8[4718592]{0:T(1024)(128)(4,1)} %bitcast.110), calls=%async_computation.4 | async-start | bytes 1048576
  597.8 8.1 %copy-start.1 = (bf16[768,768]{1,0:T(8,128)(2,1)S(1)}, bf16[768,768]{1,0:T(8,128)(2,1)}, u32[]{:S(2)}) copy-start(bf16[768,768]{1,0:T(8,128)(2,1)} %param.32) | copy-start | bytes 3538948
  597.8 7.2 %copy-start.25 = (bf16[192,768]{1,0:T(8,128)(2,1)S(1)}, bf16[192,768]{1,0:T(8,128)(2,1)}, u32[]{:S(2)}) copy-start(bf16[192,768]{1,0:T(8,128)(2,1)} %get-tuple-element.231) | copy-start | bytes 884740
  (58 other events, 197.9 us)
Sparse Core Ops, SparseCore 0:
  72.6 58.3 all-reduce.7
  159.5 55.7 all-reduce.9
  358.9 94.1 all-reduce.13
  458.0 139.6 all-reduce.11
where the time goes:
time: 620 us; the launch traced here: 613 us
  waiting for transfers between devices  269 us (43%)
  matrix products  139 us (22%)
  other arithmetic  116 us (19%)
  blocking collectives  40.5 us (7%)
  local copies, waits for them, and re-layouts  29.3 us (5%)
  between operations  15.1 us (2%)
    psum x1, waiting for transfers between devices, sum_gradients(): lax.psum([g.astype(jnp.bfloat16) for g, w in zip(grads, large) if w], 'dp')  84.2 us
    psum x1, waiting for transfers between devices, run_forward(): mlp_total = lax.psum(mlp_part, 'tensor').astype(jnp.float32)  80.8 us
    psum x1, waiting for transfers between devices, run_forward(): attn_total = lax.psum(attn_part, 'tensor').astype(jnp.float32)  53.4 us
    psum x1, waiting for transfers between devices, on_device(): lax.psum(norm_grad_part.astype(jnp.bfloat16), 'tensor').astype(jnp.float32)  50.4 us
    psum x1, blocking collectives, sum_gradients(): wide = lax.psum([g for g, w in zip(grads, large) if not w], 'dp')  40.5 us
    dot_general x6, matrix products, block_scores(): jnp.einsum('qhd,khd->hqk', query_block, key_rows, preferred_element_type=...  30.4 us
    convert_element_type x3, other arithmetic, back_block(): score_grad = (weights * (weight_grad - centre)).astype(jnp.bfloat16)  28.3 us
    reduce_sum x4, other arithmetic, layer_norm(): return centred * lax.rsqrt(spread + NORM_EPS) * norm_gain + norm_shift  19.6 us
  transfers between devices with their start and end apart: 4, of which 4 were waited for; matrix products, arithmetic and copies ran while one was open for 7% of the time, Pallas kernels for 0%

commit v1 on v0

--- a/solution.py
+++ b/solution.py
@@ -146,7 +146,7 @@
     if second_pass:
         attn_total = lax.psum(attn_part, "tensor").astype(jnp.float32)
     else:
-        attn_total = lax.psum(attn_part, "tensor").astype(jnp.float32)
+        attn_total = jnp.sum(lax.all_gather(attn_part, "tensor"), axis=0).astype(jnp.float32)
     middle = hidden_in + attn_total + b_out.astype(jnp.float32)
     normed_two = layer_norm(
         middle, ln2_gain.astype(jnp.float32), ln2_shift.astype(jnp.float32)

time: 620 us -> 635 us (1.024)
  waiting for transfers between devices: 269 us -> 277 us
  other arithmetic: 116 us -> 123 us
    all_gather x0 -> x1, waiting for transfers between devices: none -> 62 us  [run_forward(): lax.all_gather(attn_part, 'tensor')]
    psum x1 -> x0, waiting for transfers between devices: 53.4 us -> none  [run_forward(): attn_total = lax.psum(attn_part, 'tensor').astype(jnp.float32)]
    reduce_sum x0 -> x1, other arithmetic: none -> 7.13 us  [run_forward(): jnp.sum(lax.all_gather(attn_part, 'tensor'), axis=0).astype(jnp.float32)]
where the time goes in v1:
time: 635 us; the launch traced here: 628 us
  waiting for transfers between devices  277 us (44%)
  matrix products  139 us (22%)
  other arithmetic  123 us (19%)
  blocking collectives  40.6 us (6%)
  local copies, waits for them, and re-layouts  29.2 us (5%)
  between operations  14.8 us (2%)
    psum x1, waiting for transfers between devices, sum_gradients(): lax.psum([g.astype(jnp.bfloat16) for g, w in zip(grads, large) if w], 'dp')  84.1 us
    psum x1, waiting for transfers between devices, run_forward(): mlp_total = lax.psum(mlp_part, 'tensor').astype(jnp.float32)  80.8 us
    all_gather x1, waiting for transfers between devices, run_forward(): lax.all_gather(attn_part, 'tensor')  62 us
    psum x1, waiting for transfers between devices, on_device(): lax.psum(norm_grad_part.astype(jnp.bfloat16), 'tensor').astype(jnp.float32)  50.3 us
    psum x1, blocking collectives, sum_gradients(): wide = lax.psum([g for g, w in zip(grads, large) if not w], 'dp')  40.6 us
    dot_general x6, matrix products, block_scores(): jnp.einsum('qhd,khd->hqk', query_block, key_rows, preferred_element_type=...  30.4 us
    convert_element_type x3, other arithmetic, back_block(): score_grad = (weights * (weight_grad - centre)).astype(jnp.bfloat16)  28.3 us
    reduce_sum x4, other arithmetic, layer_norm(): return centred * lax.rsqrt(spread + NORM_EPS) * norm_gain + norm_shift  19.9 us
  transfers between devices with their start and end apart: 4, of which 4 were waited for; matrix products, arithmetic and copies ran while one was open for 7% of the time, Pallas kernels for 0%

profile of v1, /device:TPU:0, one launch (start us, length us, event | category | flops | bytes accessed | tf_op | source)
XLA Modules:
  0.0 628.1 jit_solution(14172625536550729564)
XLA Ops:
  8.1 8.3 %multiply_sine_fusion = (f32[3,1536,128]{2,1,0:T(8,128)S(1)}, f32[3,1536,128]{2,1,0:T(8,128)S(1)}) fusion(f32[128]{0:T(128)S(1)} %negate_power_fusion, f32[3,1536]{1,0:T(4,128)S(1)} %convert_element_type.155), kind=kLoop, calls=%fused_computation.89 | loop fusion | flops 589824 | bytes 4737536 | tf_op jit(solution)/shard_map/sin | solution.py:25
  29.3 38.7 %while.27 = (s32[]{:T(128)}, bf16[3,512,3,64]{1,3,2,0:T(8,128)(2,1)S(1)}, f32[3,3,512]{2,1,0:T(4,128)}, s32[3]{0:T(128)S(1)}, s32[1536]{0:T(1024)}, /*index=5*/s...) while((s32[]{:T(128)}, ...), condition=%wide.region_7.8_spmd, body=%wide.region_4.7_spmd.sunk | while | flops 633076224 | bytes 33307488 | solution.py:64
  77.2 62.0 %all-gather.3.cloned.1.call-done = bf16[6144,768]{1,0:T(8,128)(2,1)} async-done(((bf16[1536,768]{1,0:T(8,128)(2,1)}), bf16[6144,768]{1,0:T(8,128)(2,1)}) %all-gather.3.cloned.1.call-update) | async-done | bytes 9437200 | tf_op jit(solution)/shard_map/all_gather | solution.py:149
  139.2 7.1 %reduce_sum.192 = bf16[1536,768]{1,0:T(8,128)(2,1)} reduce(bf16[4,1536,768]{2,1,0:T(8,128)(2,1)} %bitcast.116, bf16[]{:T(256)} %constant.32.clone.1), dimensions={0}, to_apply=%region_8.9 | reduce | flops 3538944 | bytes 11796482 | tf_op jit(solution)/shard_map/reduce_sum | solution.py:149
  152.4 12.8 %multiply_convert_fusion.1 = (bf16[1536,768]{1,0:T(8,128)(2,1)}, f32[1536,768]{1,0:T(8,128)S(1)}, f32[1536,768]{1,0:T(8,128)S(1)}) fusion(f32[768]{0:T(1024)S(1)} %copy-done.49, bf16[1536,768]{1,0:T(8,128)(2,1)S(1)} %add_convert_fusion.1, bf16[768,768]{1,0:T(8,128)(2,1)S(1)} %copy-done), kind=kOutput, calls=%fused_computation.69 | convolution fusion | flops 1889796096 | bytes 15338496 | tf_op jit(solution)/shard_map/dot_general | solution.py:154
  165.2 4.6 convert_reduce_fusion.3
  174.8 5.4 convolution_convert_fusion.1
  180.2 50.3 %all-reduce.7.cloned.1.call-done = bf16[1536,768]{1,0:T(8,128)(2,1)} async-done(((bf16[1536,768]{1,0:T(8,128)(2,1)}), bf16[1536,768]{1,0:T(8,128)(2,1)}) %all-reduce.7.cloned.1.call-update) | async-done | bytes 2359312 | tf_op jit(solution)/shard_map/psum | solution.py:246
  230.5 5.3 convert_reduce_fusion.1
  235.9 5.5 fusion.38
  241.4 5.2 fusion.57
  251.5 114.2 %while.28 = (s32[]{:T(128)}, f32[1536,3,64]{0,2,1:T(8,128)}, f32[1536,3,64]{0,2,1:T(8,128)S(1)}, bf16[3,512,3,64]{1,3,2,0:T(8,128)(2,1)}, s32[3]{0:T(128)S(1)}, ...) while((s32[]{:T(128)}, f32[1536,3,64]{0,2,1:T(8,128)}, ...), condition=%wide.region_17.18_spmd.clone, body=%wide.region_15.17_spmd.clone.sunk | while | flops 1533540864 | bytes 113105432 | solution.py:108
  252.6 6.0 fusion.122
  260.6 8.1 %multiply_reduce_fusion.4 = (f32[3,512]{1,0:T(4,128)S(1)}, f32[3,512,1536]{2,1,0:T(8,128)}) fusion(f32[3,512,1536]{2,1,0:T(8,128)} %fusion.122, f32[3,512]{1,0:T(4,128)S(1)} %dynamic-slice_bitcast_fusion.2, bf16[1536,3,64]{0,2,1:T(8,128)(2,1)S(1)} %get-tuple-element.476, bf16[1536,3,64]{0,2,1:T(8,128)(2,1)} %get-tuple-element.473, ...), kind=kOutput, calls=%fused_computation.16.clone.1 | convolution fusion | flops 313784832 | bytes 20459524 | tf_op jit(solution)/shard_map/while/body/eval_jaxpr/qhd,khd->hqk/dot_general | solution.py:41
  268.8 9.4 %multiply_convert_fusion.3 = bf16[3,512,1536]{2,1,0:T(8,128)(2,1)} fusion(f32[3,512,1536]{2,1,0:T(8,128)} %get-tuple-element.395, f32[3,512,1536]{2,1,0:T(8,128)} %fusion.122, f32[3,512]{1,0:T(4,128)S(1)} %get-tuple-element.396), kind=kLoop, calls=%fused_computation.15.clone.1 | loop fusion | flops 7077888 | bytes 23599104 | tf_op jit(solution)/shard_map/while/body/eval_jaxpr/convert_element_type | solution.py:87
  284.6 4.9 fusion.124
  290.7 6.0 fusion.122
  298.7 8.1 %multiply_reduce_fusion.4 = (f32[3,512]{1,0:T(4,128)S(1)}, f32[3,512,1536]{2,1,0:T(8,128)}) fusion(f32[3,512,1536]{2,1,0:T(8,128)} %fusion.122, f32[3,512]{1,0:T(4,128)S(1)} %dynamic-slice_bitcast_fusion.2, bf16[1536,3,64]{0,2,1:T(8,128)(2,1)S(1)} %get-tuple-element.476, bf16[1536,3,64]{0,2,1:T(8,128)(2,1)} %get-tuple-element.473, ...), kind=kOutput, calls=%fused_computation.16.clone.1 | convolution fusion | flops 313784832 | bytes 20459524 | tf_op jit(solution)/shard_map/while/body/eval_jaxpr/qhd,khd->hqk/dot_general | solution.py:41
  306.9 9.4 %multiply_convert_fusion.3 = bf16[3,512,1536]{2,1,0:T(8,128)(2,1)} fusion(f32[3,512,1536]{2,1,0:T(8,128)} %get-tuple-element.395, f32[3,512,1536]{2,1,0:T(8,128)} %fusion.122, f32[3,512]{1,0:T(4,128)S(1)} %get-tuple-element.396), kind=kLoop, calls=%fused_computation.15.clone.1 | loop fusion | flops 7077888 | bytes 23599104 | tf_op jit(solution)/shard_map/while/body/eval_jaxpr/convert_element_type | solution.py:87
  322.7 4.9 fusion.124
  328.8 6.0 fusion.122
  336.8 8.1 %multiply_reduce_fusion.4 = (f32[3,512]{1,0:T(4,128)S(1)}, f32[3,512,1536]{2,1,0:T(8,128)}) fusion(f32[3,512,1536]{2,1,0:T(8,128)} %fusion.122, f32[3,512]{1,0:T(4,128)S(1)} %dynamic-slice_bitcast_fusion.2, bf16[1536,3,64]{0,2,1:T(8,128)(2,1)S(1)} %get-tuple-element.476, bf16[1536,3,64]{0,2,1:T(8,128)(2,1)} %get-tuple-element.473, ...), kind=kOutput, calls=%fused_computation.16.clone.1 | convolution fusion | flops 313784832 | bytes 20459524 | tf_op jit(solution)/shard_map/while/body/eval_jaxpr/qhd,khd->hqk/dot_general | solution.py:41
  344.9 9.4 %multiply_convert_fusion.3 = bf16[3,512,1536]{2,1,0:T(8,128)(2,1)} fusion(f32[3,512,1536]{2,1,0:T(8,128)} %get-tuple-element.395, f32[3,512,1536]{2,1,0:T(8,128)} %fusion.122, f32[3,512]{1,0:T(4,128)S(1)} %get-tuple-element.396), kind=kLoop, calls=%fused_computation.15.clone.1 | loop fusion | flops 7077888 | bytes 23599104 | tf_op jit(solution)/shard_map/while/body/eval_jaxpr/convert_element_type | solution.py:87
  360.7 4.9 fusion.124
  369.6 4.6 bitcast_convert_fusion
  374.4 5.6 convolution_convert_fusion.5
  387.8 80.8 %all-reduce.11.cloned.1.call-done = (bf16[1536,768]{1,0:T(8,128)(2,1)}, bf16[1536,768]{1,0:T(8,128)(2,1)}) async-done(((bf16[1536,768]{1,0:T(8,128)(2,1)}, bf16[1536,768]{1,0:T(8,128)(2,1)}), (bf16[1536,768]{1,0:T(8,128)(2,1)}, bf16[1536,768]{1,0:T(8,128)(2,1)})) %all-reduce.11.cloned.1.call-update) | async-done | bytes 4718608 | tf_op jit(solution)/shard_map/psum | solution.py:173
  468.6 4.7 convert_reduce_fusion
  477.8 40.6 %all-reduce = (f32[768]{0:T(1024)}, f32[768]{0:T(1024)}, f32[2,192]{1,0:T(2,128)}, f32[768]{0:T(1024)}, f32[768]{0:T(1024)}, /*index=5*/f32[768]{0:T(1024)}, f32[768]{0:T(1024)}, f32[768]{0:T(1024)}) all-reduce(f32[768]{0:T(1024)S(1)} %get-tuple-element.172, ...), channel_id=1, replica_groups=mesh['dp'=8,'tensor'=4] {'dp'}, use_global_device_ids=true, to_apply=%region_22.23 | all-reduce | flops 5760 | bytes 46080 | tf_op jit(solution)/shard_map/psum | solution.py:181
  518.5 4.8 select_convert_fusion
  524.4 4.8 add_add_fusion.2
  529.2 84.1 %all-reduce.9.cloned.1.call-done = (bf16[768,3,192]{0,2,1:T(8,128)(2,1)}, bf16[192,768]{1,0:T(8,128)(2,1)}, bf16[768,768]{1,0:T(8,128)(2,1)}, bf16[768,768]{1,0:T(8,128)(2,1)}) async-done(((bf16[768,3,192]{0,2,1:T(8,128)(2,1)}, bf16[192,768]{1,0:T(8,128)(2,1)}, bf16[768,768]{1,0:T(8,128)(2,1)}, bf16[768,768]{1,0:T(8,128)(2,1)}), (bf16[768,3,192]{0,2,1:T(8,128)(2,1)}, bf16[192,768]{1,0:T(8,128)(2,1)}, ...) | async-done | bytes 3538960 | tf_op jit(solution)/shard_map/psum | solution.py:180
  (291 shorter events, 126.9 us)
Async XLA Ops:
  7.2 145.2 %copy-start = (bf16[768,768]{1,0:T(8,128)(2,1)S(1)}, bf16[768,768]{1,0:T(8,128)(2,1)}, u32[]{:S(2)}) copy-start(bf16[768,768]{1,0:T(8,128)(2,1)} %param.32) | copy-start | bytes 3538948
  7.2 132.0 %all-gather.3.cloned.1.call-start = ((), (), s32[]{:S(2)}) async-start(), calls=%async_computation.1 | async-start | bytes 11796480 | tf_op jit(solution)/shard_map/all_gather | solution.py:149
  68.0 78.4 %copy-start.8 = (bf16[1536,3,64]{0,2,1:T(8,128)(2,1)}, bf16[1536,3,64]{0,2,1:T(8,128)(2,1)S(1)}, u32[]{:S(2)}) copy-start(bf16[1536,3,64]{0,2,1:T(8,128)(2,1)S(1)} %get-tuple-element.500) | copy-start | bytes 1769476
  68.7 77.7 %copy-start.12 = (bf16[24,8,3,512]{3,1,2,0:T(8,128)(2,1)}, bf16[24,8,3,512]{3,1,2,0:T(8,128)(2,1)S(1)}, u32[]{:S(2)}) copy-start(bf16[24,8,3,512]{3,1,2,0:T(8,128)(2,1)S(1)} %copy.35) | copy-start | bytes 1769476
  72.1 158.4 %all-reduce.7.cloned.1.call-start = ((), (), s32[]{:S(2)}) async-start(), calls=%async_computation | async-start | bytes 4718592 | tf_op jit(solution)/shard_map/psum | solution.py:246
  150.9 14.3 %copy-start.38 = (f32[1536]{0:T(1024)}, f32[1536]{0:T(1024)S(1)}, u32[]{:S(2)}) copy-start(f32[1536]{0:T(1024)S(1)} %multiply_reduce_fusion.1) | copy-start | bytes 18436
  150.9 14.3 %copy-start.30 = (f32[1536]{0:T(1024)}, f32[1536]{0:T(1024)S(1)}, u32[]{:S(2)}) copy-start(f32[1536]{0:T(1024)S(1)} %fusion.53) | copy-start | bytes 18436
  152.4 12.8 %copy-start.22 = (bf16[1536,768]{1,0:T(8,128)(2,1)}, bf16[1536,768]{1,0:T(8,128)(2,1)S(1)}, u32[]{:S(2)}) copy-start(bf16[1536,768]{1,0:T(8,128)(2,1)S(1)} %add_convert_fusion.1) | copy-start | bytes 7077892
  152.4 12.8 %copy-start.17 = (bf16[1536,768]{1,0:T(8,128)(2,1)S(1)}, bf16[1536,768]{1,0:T(8,128)(2,1)}, u32[]{:S(2)}) copy-start(bf16[1536,768]{1,0:T(8,128)(2,1)} %param.23) | copy-start | bytes 7077892
  152.4 12.8 %copy-start.40 = (pred[1536]{0:T(1024)(128)(4,1)S(1)}, pred[1536]{0:T(1024)(128)(4,1)}, u32[]{:S(2)}) copy-start(pred[1536]{0:T(1024)(128)(4,1)} %iota_compare_fusion.1) | copy-start | bytes 4612
  152.4 12.8 %copy-start.55 = (bf16[768,768]{1,0:T(8,128)(2,1)S(1)}, bf16[768,768]{1,0:T(8,128)(2,1)}, u32[]{:S(2)}) copy-start(bf16[768,768]{1,0:T(8,128)(2,1)} %param.34) | copy-start | bytes 3538948
  174.7 293.9 %all-reduce.11.cloned.1.call-start = ((), (), s32[]{:S(2)}) async-start(), calls=%async_computation.3 | async-start | bytes 9437184 | tf_op jit(solution)/shard_map/psum | solution.py:173
  174.8 55.7 %copy-start.35 = (f32[768]{0:T(1024)S(1)}, f32[768]{0:T(1024)}, u32[]{:S(2)}) copy-start(f32[768]{0:T(1024)} %convert_element_type.168) | copy-start | bytes 9220
  180.2 55.7 %copy-start.39 = (f32[1536]{0:T(1024)S(1)}, f32[1536]{0:T(1024)}, u32[]{:S(2)}) copy-start(f32[1536]{0:T(1024)} %copy-done.38) | copy-start | bytes 18436
  180.2 55.7 %copy-start.31 = (f32[1536]{0:T(1024)S(1)}, f32[1536]{0:T(1024)}, u32[]{:S(2)}) copy-start(f32[1536]{0:T(1024)} %copy-done.30) | copy-start | bytes 18436
  241.4 7.5 %copy-start.23 = (bf16[192,768]{1,0:T(8,128)(2,1)S(1)}, bf16[192,768]{1,0:T(8,128)(2,1)}, u32[]{:S(2)}) copy-start(bf16[192,768]{1,0:T(8,128)(2,1)} %param.28) | copy-start | bytes 884740
  268.8 9.5 %copy-start.6 = (f32[1536,3,64]{0,2,1:T(8,128)S(1)}, f32[1536,3,64]{0,2,1:T(8,128)}, u32[]{:S(2)}) copy-start(f32[1536,3,64]{0,2,1:T(8,128)} %get-tuple-element.453) | copy-start | bytes 3538948 | tf_op jit(solution)/shard_map/while
  281.8 7.7 %copy-start.7 = (f32[1536,3,64]{0,2,1:T(8,128)}, f32[1536,3,64]{0,2,1:T(8,128)S(1)}, u32[]{:S(2)}) copy-start(f32[1536,3,64]{0,2,1:T(8,128)S(1)} %fusion.123) | copy-start | bytes 3538948 | tf_op jit(solution)/shard_map/while
  289.5 7.2 %copy-start.58 = (s32[3]{0:T(128)}, s32[3]{0:T(128)S(1)}, u32[]{:S(2)}) copy-start(s32[3]{0:T(128)S(1)} %get-tuple-element.472) | copy-start | bytes 40 | tf_op jit(solution)/shard_map/while
  306.9 9.5 %copy-start.6 = (f32[1536,3,64]{0,2,1:T(8,128)S(1)}, f32[1536,3,64]{0,2,1:T(8,128)}, u32[]{:S(2)}) copy-start(f32[1536,3,64]{0,2,1:T(8,128)} %get-tuple-element.453) | copy-start | bytes 3538948 | tf_op jit(solution)/shard_map/while
  319.9 7.7 %copy-start.7 = (f32[1536,3,64]{0,2,1:T(8,128)}, f32[1536,3,64]{0,2,1:T(8,128)S(1)}, u32[]{:S(2)}) copy-start(f32[1536,3,64]{0,2,1:T(8,128)S(1)} %fusion.123) | copy-start | bytes 3538948 | tf_op jit(solution)/shard_map/while
  327.6 7.2 %copy-start.58 = (s32[3]{0:T(128)}, s32[3]{0:T(128)S(1)}, u32[]{:S(2)}) copy-start(s32[3]{0:T(128)S(1)} %get-tuple-element.472) | copy-start | bytes 40 | tf_op jit(solution)/shard_map/while
  344.9 9.5 %copy-start.6 = (f32[1536,3,64]{0,2,1:T(8,128)S(1)}, f32[1536,3,64]{0,2,1:T(8,128)}, u32[]{:S(2)}) copy-start(f32[1536,3,64]{0,2,1:T(8,128)} %get-tuple-element.453) | copy-start | bytes 3538948 | tf_op jit(solution)/shard_map/while
  358.0 7.7 %copy-start.7 = (f32[1536,3,64]{0,2,1:T(8,128)}, f32[1536,3,64]{0,2,1:T(8,128)S(1)}, u32[]{:S(2)}) copy-start(f32[1536,3,64]{0,2,1:T(8,128)S(1)} %fusion.123) | copy-start | bytes 3538948 | tf_op jit(solution)/shard_map/while
  374.3 239.0 %all-reduce.9.cloned.1.call-start = ((), (), s32[]{:S(2)}) async-start(), calls=%async_computation.2 | async-start | bytes 7077888 | tf_op jit(solution)/shard_map/psum | solution.py:180
  386.1 82.5 %copy-start.27 = (f32[1536]{0:T(1024)S(1)}, f32[1536]{0:T(1024)}, u32[]{:S(2)}) copy-start(f32[1536]{0:T(1024)} %copy-done.26) | copy-start | bytes 18436
  386.1 82.5 %copy-start.33 = (f32[768]{0:T(1024)S(1)}, f32[768]{0:T(1024)}, u32[]{:S(2)}) copy-start(f32[768]{0:T(1024)} %copy-done.32) | copy-start | bytes 9220
  387.6 85.8 %copy-start.37 = (f32[1536]{0:T(1024)S(1)}, f32[1536]{0:T(1024)}, u32[]{:S(2)}) copy-start(f32[1536]{0:T(1024)} %copy-done.36) | copy-start | bytes 18436
  387.6 85.8 %copy-start.29 = (f32[1536]{0:T(1024)S(1)}, f32[1536]{0:T(1024)}, u32[]{:S(2)}) copy-start(f32[1536]{0:T(1024)} %copy-done.28) | copy-start | bytes 18436
  473.4 49.8 %slice-start = ((s8[4718592]{0:T(1024)(128)(4,1)}), s8[524288]{0:T(1024)(128)(4,1)S(1)}, s32[]{:S(2)}) async-start(s8[4718592]{0:T(1024)(128)(4,1)} %bitcast.111), calls=%async_computation.4 | async-start | bytes 1048576
  613.3 8.1 %copy-start.1 = (bf16[768,768]{1,0:T(8,128)(2,1)S(1)}, bf16[768,768]{1,0:T(8,128)(2,1)}, u32[]{:S(2)}) copy-start(bf16[768,768]{1,0:T(8,128)(2,1)} %param.32) | copy-start | bytes 3538948
  613.3 7.2 %copy-start.25 = (bf16[192,768]{1,0:T(8,128)(2,1)S(1)}, bf16[192,768]{1,0:T(8,128)(2,1)}, u32[]{:S(2)}) copy-start(bf16[192,768]{1,0:T(8,128)(2,1)} %get-tuple-element.231) | copy-start | bytes 884740
  (58 other events, 198.5 us)
Sparse Core Ops, SparseCore 0:
  72.2 66.9 all-gather.2
  174.8 55.6 all-reduce.6
  374.4 94.1 all-reduce.10
  473.5 139.6 all-reduce.8
